TPU v7x, 256 devices: a whole 4x4x8 slice. The times are simulated.
256 devices in a mesh: feat: 16 (over z, y_hi), ex: 16 (over y_lo, x, core).
Axes of the slice: x: 4, y: 4 (y_hi: 2, y_lo: 2; y = y_hi * 2 + y_lo), z: 8, core: 2. Of those that a mesh axis runs over, the one named last changes fastest.
Arguments:
- activations: bfloat16 [1024, 28672], P('ex', 'feat'), may hold values from -6 to 6
- out_grads: bfloat16 [1024, 8192], P('feat', 'ex'), may hold values from -6 to 6
- basis_in: bfloat16 [28672, 28672], P('feat', 'ex'), may hold values from -0.03125 to 0.03125
- basis_out: bfloat16 [8192, 8192], P('ex', 'feat'), may hold values from -0.0625 to 0.0625
Outputs:
- correction: float32 [8192, 28672], P('feat', 'ex')
All inputs are finite; a program needn't handle non-finite values.
Results may differ from a plain program's by a relative error of at most 0.0034.
Values may be sent and summed in bfloat16 or wider, within the bound.
A program may use at most 64 MiB of HBM per device.

v0:
```python
import jax
import jax.numpy as jnp
from jax import lax
from jax.sharding import PartitionSpec as P

SEQ_LEN = 256


def per_device(activations, out_grads, basis_in, basis_out):
    partial_in = jnp.dot(
        lax.all_gather(activations, "ex", axis=0, tiled=True),
        basis_in,
        preferred_element_type=jnp.float32,
    )
    rotated_in = lax.psum(partial_in, "feat").astype(jnp.bfloat16)
    grad_all = lax.all_gather(out_grads, "feat", axis=0, tiled=True)
    out_share = lax.psum_scatter(
        jnp.dot(grad_all, basis_out, preferred_element_type=jnp.float32),
        "ex",
        scatter_dimension=0,
        tiled=True,
    )
    rotated_out = lax.all_gather(out_share.astype(jnp.bfloat16), "ex", axis=0, tiled=True)
    tokens_all = rotated_in.shape[0]
    seq_count = tokens_all // SEQ_LEN
    in_blocks = rotated_in.reshape(seq_count, SEQ_LEN, rotated_in.shape[1])
    out_blocks = rotated_out.reshape(seq_count, SEQ_LEN, rotated_out.shape[1])
    per_seq = jnp.einsum("nto,nti->noi", out_blocks, in_blocks, preferred_element_type=jnp.float32)
    total = jnp.sum(per_seq * per_seq, axis=0)
    return total / jnp.float32(tokens_all)


def solution(mesh):
    return jax.shard_map(
        per_device,
        mesh=mesh,
        in_specs=(P("ex", "feat"), P("feat", "ex"), P("feat", "ex"), P("ex", "feat")),
        out_specs=P("feat", "ex"),
        check_vma=False,
    )
```

profile of v0, /device:TPU:2, one launch (start us, length us, event | category | flops | bytes accessed | tf_op | source)
XLA Modules:
  0.0 540.3 jit_solution(13047750849756554427)
XLA Ops:
  6.5 0.0 copy-start
  6.5 0.0 all-gather.4.cloned.1.call-start
  6.5 0.7 all-gather.4.cloned.1.call-update
  7.3 0.0 reduce-scatter.2.cloned.1.call-start
  7.3 84.3 %all-gather.4.cloned.1.call-done = bf16[1024,512]{1,0:T(8,128)(2,1)} async-done(((bf16[64,512]{1,0:T(8,128)(2,1)}), bf16[1024,512]{1,0:T(8,128)(2,1)}) %all-gather.4.cloned.1.call-update) | async-done | bytes 1048592 | tf_op jit(solution)/shard_map/all_gather | solution.py:16
  91.7 0.0 copy-done
  91.7 3.2 fusion
  94.9 0.0 reduce-scatter.2.cloned.1.call-update
  94.9 0.0 all-gather.8.cloned.1.call-start
  95.0 0.7 all-gather.8.cloned.1.call-update
  95.7 0.0 all-gather.6.cloned.1.call-start
  95.7 58.4 %reduce-scatter.2.cloned.1.call-done = f32[64,512]{1,0:T(8,128)} async-done(((f32[1024,512]{1,0:T(8,128)}), f32[64,512]{1,0:T(8,128)}) %reduce-scatter.2.cloned.1.call-update) | async-done | bytes 131088 | tf_op jit(solution)/shard_map/reduce_scatter | solution.py:17
  154.1 1.5 convert_element_type.6
  155.7 0.0 all-gather.6.cloned.1.call-update
  155.7 41.8 %all-gather.8.cloned.1.call-done = bf16[1024,1792]{1,0:T(8,128)(2,1)} async-done(((bf16[64,1792]{1,0:T(8,128)(2,1)}), bf16[1024,1792]{1,0:T(8,128)(2,1)}) %all-gather.8.cloned.1.call-update) | async-done | bytes 3670032 | tf_op jit(solution)/shard_map/all_gather | solution.py:11
  197.4 12.2 %fusion.1 = f32[1024,1792]{1,0:T(8,128)} fusion(bf16[1024,1792]{1,0:T(8,128)(2,1)} %all-gather.8.cloned.1.call-done, bf16[1792,1792]{1,0:T(8,128)(2,1)} %param.6), kind=kOutput, calls=%fused_computation.3 | convolution fusion | flops 6576668672 | bytes 17432576 | tf_op jit(solution)/shard_map/dot_general | solution.py:10
  209.6 317.3 %all-reduce.1 = bf16[1024,1792]{1,0:T(8,128)(2,1)} all-reduce(f32[1024,1792]{1,0:T(8,128)} %fusion.1), channel_id=1, replica_groups=mesh['feat'=16,'ex'=16] {'feat'}, use_global_device_ids=true, to_apply=%region_1.0 | all-reduce | flops 1835008 | bytes 11010048 | tf_op jit(solution)/shard_map/psum | solution.py:15
  526.9 0.0 all-gather.6.cloned.1.call-done
  526.9 4.8 multiply_reduce_fusion
  531.7 2.1 broadcast_multiply_fusion
Async XLA Ops:
  6.5 85.1 %copy-start = (bf16[512,512]{1,0:T(8,128)(2,1)S(1)}, bf16[512,512]{1,0:T(8,128)(2,1)}, u32[]{:S(2)}) copy-start(bf16[512,512]{1,0:T(8,128)(2,1)} %param.7) | copy-start | bytes 1572868
  6.5 85.1 %all-gather.4.cloned.1.call-start = ((), (), s32[]{:S(2)}) async-start(), calls=%async_computation.1 | async-start | bytes 1114112 | tf_op jit(solution)/shard_map/all_gather | solution.py:16
  7.3 146.9 %reduce-scatter.2.cloned.1.call-start = ((), (), s32[]{:S(2)}) async-start(), calls=%async_computation.2 | async-start | bytes 2228224 | tf_op jit(solution)/shard_map/reduce_scatter | solution.py:17
  94.9 102.5 %all-gather.8.cloned.1.call-start = ((), (), s32[]{:S(2)}) async-start(), calls=%async_computation.4 | async-start | bytes 3899392 | tf_op jit(solution)/shard_map/all_gather | solution.py:11
  95.7 431.2 %all-gather.6.cloned.1.call-start = ((), (), s32[]{:S(2)}) async-start(), calls=%async_computation.3 | async-start | bytes 1114112 | tf_op jit(solution)/shard_map/all_gather | solution.py:23
Sparse Core Ops, SparseCore 0:
  9.9 81.6 all-gather.3
  95.0 59.0 reduce-scatter.1
  156.0 41.4 all-gather.7
  199.1 46.5 all-gather.5
where the time goes:
time: 540 us
  blocking collectives  317 us (59%)
  waiting for transfers between devices  186 us (34%)
  matrix products  20.2 us (4%)
  between operations  13.1 us (2%)
    psum x1, blocking collectives, per_device(): rotated_in = lax.psum(partial_in, 'feat').astype(jnp.bfloat16)  317 us
    all_gather x1, waiting for transfers between devices, per_device(): grad_all = lax.all_gather(out_grads, 'feat', axis=0, tiled=True)  84.3 us
    reduce_scatter x1, waiting for transfers between devices, per_device(): lax.psum_scatter(jnp.dot(grad_all, basis_out, preferred_element_type=jnp....  58.4 us
    all_gather x1, waiting for transfers between devices, per_device(): lax.all_gather(activations, 'ex', axis=0, tiled=True)  41.8 us
    dot_general x1, matrix products, per_device(): jnp.dot(lax.all_gather(activations, 'ex', axis=0, tiled=True), basis_in,...  12.2 us
  transfers between devices with their start and end apart: 4, of which 3 were waited for; matrix products, arithmetic and copies ran while one was open for 3% of the time, Pallas kernels for 0%

commit v1 on v0

--- a/solution.py
+++ b/solution.py
@@ -6,11 +6,16 @@
 SEQ_LEN = 256
 
 
+def all_by_exchange(x, name, d):
+    n_dev = lax.axis_size(name)
+    parts = jnp.stack([x for _ in range(n_dev)])
+    parts = lax.all_to_all(parts, name, split_axis=0, concat_axis=0)
+    return jnp.concatenate(parts, axis=d)
+
+
 def per_device(activations, out_grads, basis_in, basis_out):
     partial_in = jnp.dot(
-        lax.all_gather(activations, "ex", axis=0, tiled=True),
-        basis_in,
-        preferred_element_type=jnp.float32,
+        all_by_exchange(activations, "ex", 0), basis_in, preferred_element_type=jnp.float32
     )
     rotated_in = lax.psum(partial_in, "feat").astype(jnp.bfloat16)
     grad_all = lax.all_gather(out_grads, "feat", axis=0, tiled=True)

time: 540 us -> 498 us (0.922)
  the two profiles are of different devices: /device:TPU:2 before, /device:TPU:30 now
where the time goes in v1:
time: 498 us
  blocking collectives  317 us (64%)
  waiting for transfers between devices  135 us (27%)
  matrix products  20.3 us (4%)
  between operations  13.1 us (3%)
  starting transfers between devices  5.78 us (1%)
    psum x1, blocking collectives, per_device(): rotated_in = lax.psum(partial_in, 'feat').astype(jnp.bfloat16)  317 us
    all_gather x1, waiting for transfers between devices, per_device(): grad_all = lax.all_gather(out_grads, 'feat', axis=0, tiled=True)  85.5 us
    reduce_scatter x1, waiting for transfers between devices, per_device(): lax.psum_scatter(jnp.dot(grad_all, basis_out, preferred_element_type=jnp....  48.5 us
    dot_general x1, matrix products, per_device(): jnp.dot(all_by_exchange(activations, 'ex', 0), basis_in, preferred_elemen...  12.2 us
  transfers between devices with their start and end apart: 4, of which 2 were waited for; matrix products, arithmetic and copies ran while one was open for 4% of the time, Pallas kernels for 0%

profile of v1, /device:TPU:30, one launch (start us, length us, event | category | flops | bytes accessed | tf_op | source)
XLA Modules:
  0.0 497.7 jit_solution(15668292720832280003)
XLA Ops:
  6.5 0.0 copy-start
  6.5 0.0 all-gather.3.cloned.1.call-start
  6.5 0.7 all-gather.3.cloned.1.call-update
  7.3 3.1 stack.2
  10.4 5.7 %all-to-all-start = ((bf16[16,64,1792]{2,1,0:T(8,128)(2,1)}), bf16[16,64,1792]{2,1,0:T(8,128)(2,1)}, u32[]{:S(2)}, u32[]{:S(2)}) async-start(bf16[16,64,1792]{2,1,0:T(8,128)(2,1)} %stack.2), calls=%async_computation.1 | async-start | bytes 7340032 | tf_op jit(solution)/shard_map/all_to_all | solution.py:12
  16.1 0.0 reduce-scatter.2.cloned.1.call-start
  16.1 85.5 %all-gather.3.cloned.1.call-done = bf16[1024,512]{1,0:T(8,128)(2,1)} async-done(((bf16[64,512]{1,0:T(8,128)(2,1)}), bf16[1024,512]{1,0:T(8,128)(2,1)}) %all-gather.3.cloned.1.call-update) | async-done | bytes 1048592 | tf_op jit(solution)/shard_map/all_gather | solution.py:21
  101.6 0.0 copy-done
  101.6 3.3 fusion
  104.9 0.0 reduce-scatter.2.cloned.1.call-update
  104.9 0.0 all-gather.5.cloned.1.call-start
  105.0 0.0 all-to-all-done
  105.0 12.2 %fusion.1 = f32[1024,1792]{1,0:T(8,128)} fusion(bf16[1024,1792]{1,0:T(8,128)(2,1)} %bitcast.1, bf16[1792,1792]{1,0:T(8,128)(2,1)} %param.6), kind=kOutput, calls=%fused_computation.3 | convolution fusion | flops 6576668672 | bytes 17432576 | tf_op jit(solution)/shard_map/dot_general | solution.py:17
  117.2 48.5 %reduce-scatter.2.cloned.1.call-done = f32[64,512]{1,0:T(8,128)} async-done(((f32[1024,512]{1,0:T(8,128)}), f32[64,512]{1,0:T(8,128)}) %reduce-scatter.2.cloned.1.call-update) | async-done | bytes 131088 | tf_op jit(solution)/shard_map/reduce_scatter | solution.py:22
  165.7 1.5 convert_element_type.6
  167.2 0.0 all-gather.5.cloned.1.call-update
  167.2 317.1 %all-reduce.1 = bf16[1024,1792]{1,0:T(8,128)(2,1)} all-reduce(f32[1024,1792]{1,0:T(8,128)} %fusion.1), channel_id=1, replica_groups=mesh['feat'=16,'ex'=16] {'feat'}, use_global_device_ids=true, to_apply=%region_1.0 | all-reduce | flops 1835008 | bytes 11010048 | tf_op jit(solution)/shard_map/psum | solution.py:20
  484.4 0.0 all-gather.5.cloned.1.call-done
  484.4 4.8 multiply_reduce_fusion
  489.1 2.1 broadcast_multiply_fusion
Async XLA Ops:
  6.5 95.1 %copy-start = (bf16[512,512]{1,0:T(8,128)(2,1)S(1)}, bf16[512,512]{1,0:T(8,128)(2,1)}, u32[]{:S(2)}) copy-start(bf16[512,512]{1,0:T(8,128)(2,1)} %param.7) | copy-start | bytes 1572868
  6.5 95.1 %all-gather.3.cloned.1.call-start = ((), (), s32[]{:S(2)}) async-start(), calls=%async_computation.2 | async-start | bytes 1114112 | tf_op jit(solution)/shard_map/all_gather | solution.py:21
  10.4 94.6 %all-to-all-start = ((bf16[16,64,1792]{2,1,0:T(8,128)(2,1)}), bf16[16,64,1792]{2,1,0:T(8,128)(2,1)}, u32[]{:S(2)}, u32[]{:S(2)}) async-start(bf16[16,64,1792]{2,1,0:T(8,128)(2,1)} %stack.2), calls=%async_computation.1 | async-start | bytes 7340032 | tf_op jit(solution)/shard_map/all_to_all | solution.py:12
  16.1 149.6 %reduce-scatter.2.cloned.1.call-start = ((), (), s32[]{:S(2)}) async-start(), calls=%async_computation.3 | async-start | bytes 2228224 | tf_op jit(solution)/shard_map/reduce_scatter | solution.py:22
  104.9 379.4 %all-gather.5.cloned.1.call-start = ((), (), s32[]{:S(2)}) async-start(), calls=%async_computation.4 | async-start | bytes 1114112 | tf_op jit(solution)/shard_map/all_gather | solution.py:28
Sparse Core Ops, SparseCore 0:
  9.9 91.6 all-gather.2
  105.0 60.5 reduce-scatter.1
  167.5 43.4 all-gather.4
